TPU v7x, 32 devices: a whole 2x2x4 slice. The times are simulated.
32 devices in a mesh: grp: 2 (over y), pair: 4 (over z), aux: 2 (over x), rep: 2 (over core).
Axes of the slice: x: 2, y: 2, z: 4, core: 2. Of those that a mesh axis runs over, the one named last changes fastest.
Arguments:
- three_center: bfloat16 [5120, 4, 8000], P(('grp', 'aux', 'rep', 'pair')), parts along dimension 0, may hold values from -0.050591038 to 0.050591038
- eps_occ: float32 [8], P('grp'), parts along dimension 0, may hold values from -1.2 to -0.4
- eps_virt: float32 [16000], P(('grp', 'pair')), parts along dimension 0, may hold values from 0.2 to 3
- freq: float32 [2], P('grp'), parts along dimension 0, may hold values from 0.2 to 2
Outputs:
- polar: float32 [5120, 2560], P(('grp', 'aux', 'rep'), 'pair'), parts along dimension 0
There are 2 independent parts, one for each index of `grp`. A program takes and returns all parts, laid end to end along the dimension named above; each array names one. Nothing has to cross between parts.
All inputs are finite; a program needn't handle non-finite values.
Results may differ from a plain program's by a relative error of at most 0.0003.
Values may be sent and summed in bfloat16 or wider, within the bound.
A program may use at most 192 MiB of HBM per device.

v0:
```python
import jax
import jax.numpy as jnp
from jax import lax
from jax.sharding import PartitionSpec as P


def local(three_center, eps_occ, eps_virt, freq):
    arrived = lax.all_to_all(three_center, "pair", split_axis=2, concat_axis=0, tiled=True)
    excite = eps_virt[None, :] - eps_occ[:, None]
    weight = 2.0 * excite / (excite * excite + freq[0] * freq[0])
    height = arrived.shape[0]
    scaled = (
        (arrived.astype(jnp.float32) * weight[None, :, :]).astype(jnp.bfloat16).reshape(height, -1)
    )
    plain_rows = arrived.reshape(height, -1)
    partial_sums = lax.dot_general(
        scaled,
        lax.all_gather(plain_rows, ("aux", "rep"), axis=0, tiled=True),
        (((1,), (1,)), ((), ())),
        preferred_element_type=jnp.float32,
    )
    return lax.psum_scatter(partial_sums, "pair", scatter_dimension=1, tiled=True)


def solution(mesh):
    return jax.shard_map(
        local,
        mesh=mesh,
        in_specs=(
            P(("grp", "aux", "rep", "pair"), None, None),
            P("grp"),
            P(("grp", "pair")),
            P("grp"),
        ),
        out_specs=P(("grp", "aux", "rep"), "pair"),
        check_vma=False,
    )
```

profile of v0, /device:TPU:0, one launch (start us, length us, event | category | flops | bytes accessed | tf_op | source)
XLA Modules:
  0.0 865.8 jit_solution(16826013014737475002)
XLA Ops:
  6.5 0.0 copy-start
  6.5 0.0 all-gather.2.cloned.1.call-start
  6.5 32.8 %copy.8 = bf16[160,4,8000]{0,1,2:T(4,128)(2,1)} copy(bf16[160,4,8000]{2,1,0:T(4,128)(2,1)} %param.4) | data formatting | bytes 20480000 | tf_op args[0]
  39.3 367.0 %all_to_all.18 = bf16[160,4,8000]{0,1,2:T(4,128)(2,1)} all-to-all(bf16[160,4,8000]{0,1,2:T(4,128)(2,1)} %copy.8), channel_id=1, replica_groups=mesh['grp'=2,'pair'=4,'aux'=2,'rep'=2] {'pair'}, dimensions={2} | all-to-all | bytes 20480000 | tf_op jit(solution)/shard_map/all_to_all | solution.py:8
  406.3 35.7 %copy.9 = bf16[160,4,4,2000]{3,1,0,2:T(4,128)(2,1)} copy(bf16[160,4,4,2000]{0,1,3,2:T(4,128)(2,1)} %bitcast.4) | data formatting | bytes 20480000 | tf_op jit(solution)/shard_map/all_to_all | solution.py:8
  442.0 0.0 copy-start.2
  442.0 20.3 %all_to_all.16 = bf16[640,8000]{1,0:T(8,128)(2,1)} reshape(bf16[4,160,4,2000]{3,2,1,0:T(4,128)(2,1)} %bitcast.5) | data formatting | bytes 20480000 | tf_op jit(solution)/shard_map/all_to_all | solution.py:8
  462.3 0.0 all-gather.2.cloned.1.call-update
  462.3 0.0 reduce-scatter.2.cloned.1.call-start
  463.0 0.0 copy-done
  463.1 0.1 broadcast_reduce_fusion
  463.2 0.1 sub.24
  463.3 0.0 copy-done.2
  463.3 0.1 sub.22
  463.4 245.1 %all-gather.2.cloned.1.call-done = bf16[2560,8000]{1,0:T(8,128)(2,1)} async-done(((bf16[640,8000]{1,0:T(8,128)(2,1)}), bf16[2560,8000]{1,0:T(8,128)(2,1)}) %all-gather.2.cloned.1.call-update) | async-done | bytes 40960016 | tf_op jit(solution)/shard_map/all_gather | solution.py:18
  708.5 0.0 copy-start.1
  708.5 35.3 %fusion = f32[640,2560]{1,0:T(8,128)} fusion(bf16[2560,8000]{1,0:T(8,128)(2,1)} %all-gather.2.cloned.1.call-done, bf16[640,8000]{1,0:T(8,128)(2,1)} %all_to_all.16, f32[8000]{0:T(1024)S(1)} %add_divide_fusion), kind=kOutput, calls=%fused_computation.1 | convolution fusion | flops 26229760000 | bytes 57785600 | tf_op jit(solution)/shard_map/dot_general | solution.py:16
  743.8 0.0 reduce-scatter.2.cloned.1.call-update
  743.8 115.2 %reduce-scatter.2.cloned.1.call-done = f32[640,640]{1,0:T(8,128)} async-done(((f32[640,2560]{1,0:T(8,128)}), f32[640,640]{1,0:T(8,128)}) %reduce-scatter.2.cloned.1.call-update) | async-done | bytes 1638416 | tf_op jit(solution)/shard_map/reduce_scatter | solution.py:22
  859.0 0.0 copy-done.1
  (2 shorter events, 0.0 us)
Async XLA Ops:
  6.5 456.5 %copy-start = (f32[4]{0:T(128)S(1)}, f32[4]{0:T(128)}, u32[]{:S(2)}) copy-start(f32[4]{0:T(128)} %param.5) | copy-start | bytes 52
  6.5 701.9 %all-gather.2.cloned.1.call-start = ((), (), s32[]{:S(2)}) async-start(), calls=%async_computation.2 | async-start | bytes 51609600 | tf_op jit(solution)/shard_map/all_gather | solution.py:18
  442.0 21.3 %copy-start.2 = (f32[2000]{0:T(1024)S(1)}, f32[2000]{0:T(1024)}, u32[]{:S(2)}) copy-start(f32[2000]{0:T(1024)} %param.6) | copy-start | bytes 24004
  462.3 396.6 %reduce-scatter.2.cloned.1.call-start = ((), (), s32[]{:S(2)}) async-start(), calls=%async_computation.3 | async-start | bytes 8192000 | tf_op jit(solution)/shard_map/reduce_scatter | solution.py:22
  708.5 150.5 %copy-start.1 = (f32[4]{0:T(128)S(1)}, f32[4]{0:T(128)}, u32[]{:S(2)}) copy-start(f32[4]{0:T(128)} %param.5) | copy-start | bytes 52
Sparse Core Ops, SparseCore 0:
  462.5 245.9 all-gather.1
  744.0 115.0 reduce-scatter.1
where the time goes:
time: 869 us; the launch traced here: 866 us
  blocking collectives  367 us (42%)
  waiting for transfers between devices  360 us (41%)
  local copies, waits for them, and re-layouts  89.1 us (10%)
  matrix products  35.3 us (4%)
  between operations  14.1 us (2%)
    all_to_all x1, blocking collectives, local(): lax.all_to_all(three_center, 'pair', split_axis=2, concat_axis=0, tiled=T...  367 us
    all_gather x1, waiting for transfers between devices, local(): lax.all_gather(plain_rows, ('aux', 'rep'), axis=0, tiled=True)  245 us
    reduce_scatter x1, waiting for transfers between devices, local(): lax.psum_scatter(partial_sums, 'pair', scatter_dimension=1, tiled=True)  115 us
    all_to_all x2, local copies, waits for them, and re-layouts, local(): lax.all_to_all(three_center, 'pair', split_axis=2, concat_axis=0, tiled=T...  56 us
    dot_general x1, matrix products, local(): lax.dot_general(scaled, lax.all_gather(plain_rows, ('aux', 'rep'), axis=0...  35.3 us
    unnamed x7, local copies, waits for them, and re-layouts  32.8 us
  transfers between devices with their start and end apart: 2, of which 2 were waited for; matrix products, arithmetic and copies ran while one was open for 0% of the time, Pallas kernels for 0%

commit v1 on v0

--- a/solution.py
+++ b/solution.py
@@ -5,7 +5,12 @@
 
 
 def local(three_center, eps_occ, eps_virt, freq):
-    arrived = lax.all_to_all(three_center, "pair", split_axis=2, concat_axis=0, tiled=True)
+    arrived = jnp.concatenate(
+        lax.all_to_all(
+            jnp.stack(jnp.split(three_center, lax.axis_size("pair"), axis=2)), "pair", 0, 0
+        ),
+        axis=0,
+    )
     excite = eps_virt[None, :] - eps_occ[:, None]
     weight = 2.0 * excite / (excite * excite + freq[0] * freq[0])
     height = arrived.shape[0]

time: 869 us -> 689 us (0.79)
  blocking collectives: 367 us -> 234 us
  local copies, waits for them, and re-layouts: 89.1 us -> 34.1 us
  other arithmetic: 0.02 us -> 9.79 us
    all_to_all x1, blocking collectives: 367 us -> 234 us  [local(): lax.all_to_all(jnp.stack(jnp.split(three_center, lax.axis_size('pair'), a...]
    all_to_all x2 -> x0, local copies, waits for them, and re-layouts: 56 us -> none  [local(): lax.all_to_all(three_center, 'pair', split_axis=2, concat_axis=0, tiled=T...]
    unnamed x7 -> x6, local copies, waits for them, and re-layouts: 32.8 us -> 0.01 us
    reshape x0 -> x1, local copies, waits for them, and re-layouts: none -> 20.3 us  [local(): jnp.concatenate(lax.all_to_all(jnp.stack(jnp.split(three_center, lax.axis...]
    another operation x0 -> x1, local copies, waits for them, and re-layouts: none -> 13.5 us  [local(): jnp.stack(jnp.split(three_center, lax.axis_size('pair'), axis=2))]
    another operation x0 -> x1, other arithmetic: none -> 9.78 us  [local(): jnp.stack(jnp.split(three_center, lax.axis_size('pair'), axis=2))]
where the time goes in v1:
time: 689 us; the launch traced here: 688 us
  waiting for transfers between devices  361 us (52%)
  blocking collectives  234 us (34%)
  matrix products  35.4 us (5%)
  local copies, waits for them, and re-layouts  34.1 us (5%)
  between operations  14.1 us (2%)
  other arithmetic  9.79 us (1%)
    all_gather x1, waiting for transfers between devices, local(): lax.all_gather(plain_rows, ('aux', 'rep'), axis=0, tiled=True)  245 us
    all_to_all x1, blocking collectives, local(): lax.all_to_all(jnp.stack(jnp.split(three_center, lax.axis_size('pair'), a...  234 us
    reduce_scatter x1, waiting for transfers between devices, local(): lax.psum_scatter(partial_sums, 'pair', scatter_dimension=1, tiled=True)  115 us
    dot_general x1, matrix products, local(): lax.dot_general(scaled, lax.all_gather(plain_rows, ('aux', 'rep'), axis=0...  35.4 us
    reshape x1, local copies, waits for them, and re-layouts, local(): jnp.concatenate(lax.all_to_all(jnp.stack(jnp.split(three_center, lax.axis...  20.3 us
  transfers between devices with their start and end apart: 2, of which 2 were waited for; matrix products, arithmetic and copies ran while one was open for 0% of the time, Pallas kernels for 0%

profile of v1, /device:TPU:0, one launch (start us, length us, event | category | flops | bytes accessed | tf_op | source)
XLA Modules:
  0.0 688.5 jit_solution(14303969859998400281)
XLA Ops:
  6.5 0.0 copy-start
  6.5 0.0 all-gather.2.cloned.1.call-start
  6.5 13.5 %slice_bitcast_fusion.3 = (bf16[1,160,4,2000]{3,2,1,0:T(4,128)(2,1)S(1)}, bf16[1,160,4,2000]{3,2,1,0:T(4,128)(2,1)S(1)}, bf16[1,160,4,2000]{3,2,1,0:T(4,128)(2,1)S(1)}, bf16[1,160,4,2000]{3,2,1,0:T(4,128)(2,1)S(1)}) fusion(bf16[160,4,8000]{2,1,0:T(4,128)(2,1)} %param.4), kind=kLoop, calls=%fused_computation.7 | loop fusion | bytes 20480000 | tf_op jit(solution)/shard_map/stack | solution.py:10
  20.0 9.8 %pad_maximum_fusion = bf16[4,160,4,2000]{3,2,1,0:T(4,128)(2,1)S(1)} fusion(bf16[1,160,4,2000]{3,2,1,0:T(4,128)(2,1)S(1)} %get-tuple-element.7, bf16[1,160,4,2000]{3,2,1,0:T(4,128)(2,1)S(1)} %get-tuple-element.8, bf16[1,160,4,2000]{3,2,1,0:T(4,128)(2,1)S(1)} %get-tuple-element.6, bf16[1,160,4,2000]{3,2,1,0:T(4,128)(2,1)S(1)} %get-tuple-element.5), kind=kLoop, calls=%fused_computation.1 | loop fusion | flops 15360000 | bytes 20480000 | tf_op jit(solution)/shard_map/stack | solution.py:10
  29.8 234.2 %all_to_all.5 = bf16[4,160,4,2000]{3,2,1,0:T(4,128)(2,1)} all-to-all(bf16[4,160,4,2000]{3,2,1,0:T(4,128)(2,1)S(1)} %pad_maximum_fusion), channel_id=1, replica_groups=mesh['grp'=2,'pair'=4,'aux'=2,'rep'=2] {'pair'}, dimensions={0} | all-to-all | bytes 20480000 | tf_op jit(solution)/shard_map/all_to_all | solution.py:9
  264.0 20.3 %reshape.35 = bf16[640,8000]{1,0:T(8,128)(2,1)} reshape(bf16[4,160,4,2000]{3,2,1,0:T(4,128)(2,1)} %all_to_all.5) | data formatting | bytes 20480000 | tf_op jit(solution)/shard_map/reshape | solution.py:8
  284.3 0.0 copy-start.2
  284.3 0.0 all-gather.2.cloned.1.call-update
  284.4 0.2 reduce-scatter.2.cloned.1.call-start
  285.2 0.0 copy-done
  285.3 0.1 broadcast_reduce_fusion
  285.4 0.1 sub.24
  285.5 0.0 copy-done.2
  285.5 0.1 sub.22
  285.6 245.5 %all-gather.2.cloned.1.call-done = bf16[2560,8000]{1,0:T(8,128)(2,1)} async-done(((bf16[640,8000]{1,0:T(8,128)(2,1)}), bf16[2560,8000]{1,0:T(8,128)(2,1)}) %all-gather.2.cloned.1.call-update) | async-done | bytes 40960016 | tf_op jit(solution)/shard_map/all_gather | solution.py:23
  531.1 0.0 copy-start.1
  531.1 35.4 %fusion = f32[640,2560]{1,0:T(8,128)} fusion(bf16[2560,8000]{1,0:T(8,128)(2,1)} %all-gather.2.cloned.1.call-done, bf16[640,8000]{1,0:T(8,128)(2,1)} %reshape.35, f32[8000]{0:T(1024)S(1)} %add_divide_fusion), kind=kOutput, calls=%fused_computation.2 | convolution fusion | flops 26229760000 | bytes 57785600 | tf_op jit(solution)/shard_map/dot_general | solution.py:21
  566.4 0.0 reduce-scatter.2.cloned.1.call-update
  566.5 115.2 %reduce-scatter.2.cloned.1.call-done = f32[640,640]{1,0:T(8,128)} async-done(((f32[640,2560]{1,0:T(8,128)}), f32[640,640]{1,0:T(8,128)}) %reduce-scatter.2.cloned.1.call-update) | async-done | bytes 1638416 | tf_op jit(solution)/shard_map/reduce_scatter | solution.py:27
  681.6 0.0 copy-done.1
  (2 shorter events, 0.0 us)
Async XLA Ops:
  6.5 278.7 %copy-start = (f32[4]{0:T(128)S(1)}, f32[4]{0:T(128)}, u32[]{:S(2)}) copy-start(f32[4]{0:T(128)} %param.5) | copy-start | bytes 52
  6.5 524.5 %all-gather.2.cloned.1.call-start = ((), (), s32[]{:S(2)}) async-start(), calls=%async_computation.2 | async-start | bytes 51609600 | tf_op jit(solution)/shard_map/all_gather | solution.py:23
  284.3 1.1 copy-start.2
  284.4 397.3 %reduce-scatter.2.cloned.1.call-start = ((), (), s32[]{:S(2)}) async-start(), calls=%async_computation.3 | async-start | bytes 8192000 | tf_op jit(solution)/shard_map/reduce_scatter | solution.py:27
  531.1 150.6 %copy-start.1 = (f32[4]{0:T(128)S(1)}, f32[4]{0:T(128)}, u32[]{:S(2)}) copy-start(f32[4]{0:T(128)} %param.5) | copy-start | bytes 52
Sparse Core Ops, SparseCore 0:
  284.5 246.5 all-gather.1
  566.6 115.0 reduce-scatter.1
